TPU v7x, 32 devices: a whole 2x2x4 slice. The times are simulated.
32 devices in a mesh: gx: 16 (over z, x, core), gy: 2 (over y).
Axes of the slice: x: 2, y: 2, z: 4, core: 2. Of those that a mesh axis runs over, the one named last changes fastest.
Arguments:
- vectors: bfloat16 [64, 16, 128, 128], P('gx', 'gy'), may hold values from -6 to 6
- hamiltonian: bfloat16 [64, 16, 9, 128, 128], P('gx', 'gy'), may hold values from -0.125 to 0.125
- neighbours: int32 [64, 16, 9], P('gx', 'gy'), may hold values from 0 to 8, each once within a row
Outputs:
- filtered: float32 [64, 16, 128, 128], P('gx', 'gy')
Inputs may be any that keep to these rules, and one draw needn't show every extreme that they name: `neighbours`: each cell's list names every offset code 0 to 8 exactly once, in any order.
All inputs are finite; a program needn't handle non-finite values.
Results may differ from a plain program's by a relative error of at most 0.0034.
Values may be sent and summed in bfloat16 or wider, within the bound.
A program may use at most 128 MiB of HBM per device.

v0:
```python
import jax
import jax.numpy as jnp
from jax import lax
from jax.sharding import PartitionSpec as P

STEPS = 4
NBR = 9


def padded_2(value, sides, width):
    for axis, dim in sides:
        size, length = (lax.axis_size(axis), value.shape[dim])
        up = [(i, (i + 1) % size) for i in range(size)]
        down = [(j, i) for i, j in up]
        last = lax.slice_in_dim(value, length - width, length, axis=dim)
        first = lax.slice_in_dim(value, 0, width, axis=dim)
        before = lax.ppermute(last, axis, up)
        after = lax.ppermute(first, axis, down)
        value = jnp.concatenate([before, value, after], axis=dim)
    return value


def neighbour_stack(padded, cell_rows, cell_cols):
    views = []
    for offset_x in (-1, 0, 1):
        for offset_y in (-1, 0, 1):
            views.append(
                padded[
                    1 + offset_x : 1 + offset_x + cell_rows, 1 + offset_y : 1 + offset_y + cell_cols
                ]
            )
    return jnp.stack(views, axis=0)


def on_device(vectors, hamiltonian, neighbours):
    cell_rows = vectors.shape[0]
    cell_cols = vectors.shape[1]
    onehot = (neighbours[..., None] == jnp.arange(NBR, dtype=jnp.int32)).astype(jnp.bfloat16)
    ordered = jnp.einsum(
        "xyko,xykij->xyoij", onehot, hamiltonian, preferred_element_type=jnp.float32
    ).astype(jnp.bfloat16)

    def operate(current_b):
        widened = padded_2(current_b, (("gx", 0),), 1)
        padded = padded_2(widened, (("gy", 1),), 1)
        stacked = neighbour_stack(padded, cell_rows, cell_cols)
        return jnp.einsum("xyoij,oxyjm->xyim", ordered, stacked, preferred_element_type=jnp.float32)

    previous = vectors.astype(jnp.float32)
    current = operate(vectors)
    for step_index in range(1, STEPS):
        following = 2.0 * operate(current.astype(jnp.bfloat16)) - previous
        previous = current
        current = following
    return current


def solution(mesh):
    placed = (P("gx", "gy", None, None), P("gx", "gy", None, None, None), P("gx", "gy", None))
    return jax.shard_map(
        on_device, mesh=mesh, in_specs=placed, out_specs=P("gx", "gy", None, None), check_vma=False
    )
```

profile of v0, /device:TPU:0, one launch (start us, length us, event | category | flops | bytes accessed | tf_op | source)
XLA Modules:
  0.0 162.7 jit_solution(6789145237921138194)
XLA Ops:
  1.7 5.0 %collective-permute-start.1 = (bf16[1,8,128,128]{3,2,1,0:T(8,128)(2,1)S(1)}, bf16[1,8,128,128]{3,2,1,0:T(8,128)(2,1)S(1)}, u32[]{:S(2)}, u32[]{:S(2)}) collective-permute-start(bf16[1,8,128,128]{3,2,1,0:T(8,128)(2,1)S(1)} %get-tuple-element.25), channel_id=1, source_target_pairs={{2,0},{4,2},{6,4},{8,6},{10,8},{12,10},{14,12},{16,14},{18,16},{20... | collective-permute-start | bytes 786440 | tf_op jit(solution)/shard_map/ppermute | solution.py:18
  6.7 4.1 %collective-permute-done = bf16[1,8,128,128]{3,2,1,0:T(8,128)(2,1)S(1)} collective-permute-done((bf16[1,8,128,128]{3,2,1,0:T(8,128)(2,1)S(1)}, bf16[1,8,128,128]{3,2,1,0:T(8,128)(2,1)S(1)}, u32[]{:S(2)}, u32[]{:S(2)}) %collective-permute-start) | collective-permute-done | bytes 262176 | tf_op jit(solution)/shard_map/ppermute | solution.py:17
  11.1 2.1 %collective-permute-start.2 = (bf16[6,1,128,128]{3,2,1,0:T(8,128)(2,1)S(1)}, bf16[6,1,128,128]{3,2,1,0:T(8,128)(2,1)S(1)}, u32[]{:S(2)}, u32[]{:S(2)}) collective-permute-start(bf16[6,1,128,128]{3,2,1,0:T(8,128)(2,1)S(1)} %get-tuple-element.18), channel_id=1, source_target_pairs={{0,1},{1,0},{2,3},{3,2},{4,5},{5,4},{6,7},{7,6},{8,9},{9,8},{10,11... | collective-permute-start | bytes 589832 | tf_op jit(solution)/shard_map/ppermute | solution.py:17
  13.2 13.4 %fusion = bf16[4,8,9,128,128]{4,2,3,1,0:T(8,128)(2,1)} fusion(bf16[4,8,9,128,128]{4,3,2,1,0:T(8,128)(2,1)} %param.4, s32[4,8,9]{2,1,0:T(8,128)S(1)} %copy-done.3), kind=kOutput, calls=%fused_computation.1 | convolution fusion | flops 84937248 | bytes 18875520 | tf_op jit(solution)/shard_map/xyko,xykij->xyoij/dot_general | solution.py:39
  26.6 8.1 %copy.47 = bf16[4,8,9,128,128]{4,3,2,1,0:T(8,128)(2,1)S(1)} copy(bf16[4,8,9,128,128]{4,2,3,1,0:T(8,128)(2,1)} %fusion) | data formatting | bytes 18874368 | tf_op jit(solution)/shard_map/xyko,xykij->xyoij/dot_general | solution.py:39
  37.9 4.4 %collective-permute-done.3 = bf16[6,1,128,128]{3,2,1,0:T(8,128)(2,1)S(1)} collective-permute-done((bf16[6,1,128,128]{3,2,1,0:T(8,128)(2,1)S(1)}, bf16[6,1,128,128]{3,2,1,0:T(8,128)(2,1)S(1)}, u32[]{:S(2)}, u32[]{:S(2)}) %collective-permute-start.3) | collective-permute-done | bytes 196640 | tf_op jit(solution)/shard_map/ppermute | solution.py:18
  50.7 7.7 %bitcast_convert_fusion = (bf16[4,8,128,128]{3,2,1,0:T(8,128)(2,1)S(1)}, f32[4,8,128,128,1]{3,2,4,1,0:T(8,128)}) fusion(bf16[4,8,9,128,128]{4,3,2,1,0:T(8,128)(2,1)S(1)} %copy.47, bf16[9,4,8,128,128]{4,3,0,2,1:T(8,128)(2,1)} %fusion.61), kind=kOutput, calls=%fused_computation.20 | convolution fusion | flops 1208483840 | bytes 22020096 | tf_op jit(solution)/shard_map/xyoij,oxyjm->xyim/dot_general | solution.py:47
  58.6 4.3 %collective-permute-start.5 = (bf16[1,8,128,128]{3,2,1,0:T(8,128)(2,1)S(1)}, bf16[1,8,128,128]{3,2,1,0:T(8,128)(2,1)S(1)}, u32[]{:S(2)}, u32[]{:S(2)}) collective-permute-start(bf16[1,8,128,128]{3,2,1,0:T(8,128)(2,1)S(1)} %get-tuple-element.24), channel_id=1, source_target_pairs={{2,0},{4,2},{6,4},{8,6},{10,8},{12,10},{14,12},{16,14},{18,16},{20... | collective-permute-start | bytes 786440 | tf_op jit(solution)/shard_map/ppermute | solution.py:18
  62.9 4.2 %collective-permute-done.4 = bf16[1,8,128,128]{3,2,1,0:T(8,128)(2,1)S(1)} collective-permute-done((bf16[1,8,128,128]{3,2,1,0:T(8,128)(2,1)S(1)}, bf16[1,8,128,128]{3,2,1,0:T(8,128)(2,1)S(1)}, u32[]{:S(2)}, u32[]{:S(2)}) %collective-permute-start.4) | collective-permute-done | bytes 262176 | tf_op jit(solution)/shard_map/ppermute | solution.py:17
  67.2 2.0 %collective-permute-start.6 = (bf16[6,1,128,128]{3,2,1,0:T(8,128)(2,1)S(1)}, bf16[6,1,128,128]{3,2,1,0:T(8,128)(2,1)S(1)}, u32[]{:S(2)}, u32[]{:S(2)}) collective-permute-start(bf16[6,1,128,128]{3,2,1,0:T(8,128)(2,1)S(1)} %get-tuple-element.16), channel_id=1, source_target_pairs={{0,1},{1,0},{2,3},{3,2},{4,5},{5,4},{6,7},{7,6},{8,9},{9,8},{10,11... | collective-permute-start | bytes 589832 | tf_op jit(solution)/shard_map/ppermute | solution.py:17
  69.2 5.7 %collective-permute-done.7 = bf16[6,1,128,128]{3,2,1,0:T(8,128)(2,1)S(1)} collective-permute-done((bf16[6,1,128,128]{3,2,1,0:T(8,128)(2,1)S(1)}, bf16[6,1,128,128]{3,2,1,0:T(8,128)(2,1)S(1)}, u32[]{:S(2)}, u32[]{:S(2)}) %collective-permute-start.7) | collective-permute-done | bytes 196640 | tf_op jit(solution)/shard_map/ppermute | solution.py:18
  74.9 3.6 %collective-permute-done.6 = bf16[6,1,128,128]{3,2,1,0:T(8,128)(2,1)S(1)} collective-permute-done((bf16[6,1,128,128]{3,2,1,0:T(8,128)(2,1)S(1)}, bf16[6,1,128,128]{3,2,1,0:T(8,128)(2,1)S(1)}, u32[]{:S(2)}, u32[]{:S(2)}) %collective-permute-start.6) | collective-permute-done | bytes 196640 | tf_op jit(solution)/shard_map/ppermute | solution.py:17
  88.6 7.9 %fusion.76 = (bf16[4,8,128,128]{3,2,1,0:T(8,128)(2,1)S(1)}, f32[4,8,128,128]{3,2,1,0:T(8,128)}) fusion(bf16[4,8,128,128]{3,2,1,0:T(8,128)(2,1)S(1)} %copy-done.1, bf16[4,8,9,128,128]{4,3,2,1,0:T(8,128)(2,1)S(1)} %bitcast.178, bf16[9,4,8,128,128]{4,3,2,1,0:T(8,128)(2,1)} %fusion.50), kind=kOutput, calls=%fused_computation.133 | convolution fusion | flops 1210056704 | bytes 23068672 | tf_op jit(solution)/shard_map/xyoij,oxyjm->xyim/dot_general | solution.py:47
  96.6 4.4 %collective-permute-start.9 = (bf16[1,8,128,128]{3,2,1,0:T(8,128)(2,1)S(1)}, bf16[1,8,128,128]{3,2,1,0:T(8,128)(2,1)S(1)}, u32[]{:S(2)}, u32[]{:S(2)}) collective-permute-start(bf16[1,8,128,128]{3,2,1,0:T(8,128)(2,1)S(1)} %get-tuple-element.22), channel_id=1, source_target_pairs={{2,0},{4,2},{6,4},{8,6},{10,8},{12,10},{14,12},{16,14},{18,16},{20... | collective-permute-start | bytes 786440 | tf_op jit(solution)/shard_map/ppermute | solution.py:18
  101.0 4.1 %collective-permute-done.8 = bf16[1,8,128,128]{3,2,1,0:T(8,128)(2,1)S(1)} collective-permute-done((bf16[1,8,128,128]{3,2,1,0:T(8,128)(2,1)S(1)}, bf16[1,8,128,128]{3,2,1,0:T(8,128)(2,1)S(1)}, u32[]{:S(2)}, u32[]{:S(2)}) %collective-permute-start.8) | collective-permute-done | bytes 262176 | tf_op jit(solution)/shard_map/ppermute | solution.py:17
  107.2 5.6 %collective-permute-done.11 = bf16[6,1,128,128]{3,2,1,0:T(8,128)(2,1)S(1)} collective-permute-done((bf16[6,1,128,128]{3,2,1,0:T(8,128)(2,1)S(1)}, bf16[6,1,128,128]{3,2,1,0:T(8,128)(2,1)S(1)}, u32[]{:S(2)}, u32[]{:S(2)}) %collective-permute-start.11) | collective-permute-done | bytes 196640 | tf_op jit(solution)/shard_map/ppermute | solution.py:18
  112.8 2.1 %collective-permute-done.10 = bf16[6,1,128,128]{3,2,1,0:T(8,128)(2,1)S(1)} collective-permute-done((bf16[6,1,128,128]{3,2,1,0:T(8,128)(2,1)S(1)}, bf16[6,1,128,128]{3,2,1,0:T(8,128)(2,1)S(1)}, u32[]{:S(2)}, u32[]{:S(2)}) %collective-permute-start.10) | collective-permute-done | bytes 196640 | tf_op jit(solution)/shard_map/ppermute | solution.py:17
  125.2 7.1 %fusion.10 = bf16[4,8,128,128]{3,2,1,0:T(8,128)(2,1)S(1)} fusion(f32[4,8,128,128,1]{3,2,4,1,0:T(8,128)} %get-tuple-element.28, bf16[4,8,9,128,128]{4,3,2,1,0:T(8,128)(2,1)S(1)} %bitcast.178, bf16[9,4,8,128,128]{4,3,2,1,0:T(8,128)(2,1)} %fusion.40), kind=kOutput, calls=%fused_computation.17 | convolution fusion | flops 1209532416 | bytes 22020096 | tf_op jit(solution)/shard_map/xyoij,oxyjm->xyim/dot_general | solution.py:47
  132.4 4.4 %collective-permute-start.13 = (bf16[1,8,128,128]{3,2,1,0:T(8,128)(2,1)S(1)}, bf16[1,8,128,128]{3,2,1,0:T(8,128)(2,1)S(1)}, u32[]{:S(2)}, u32[]{:S(2)}) collective-permute-start(bf16[1,8,128,128]{3,2,1,0:T(8,128)(2,1)S(1)} %get-tuple-element.20), channel_id=1, source_target_pairs={{2,0},{4,2},{6,4},{8,6},{10,8},{12,10},{14,12},{16,14},{18,16},{20... | collective-permute-start | bytes 786440 | tf_op jit(solution)/shard_map/ppermute | solution.py:18
  136.9 4.0 %collective-permute-done.12 = bf16[1,8,128,128]{3,2,1,0:T(8,128)(2,1)S(1)} collective-permute-done((bf16[1,8,128,128]{3,2,1,0:T(8,128)(2,1)S(1)}, bf16[1,8,128,128]{3,2,1,0:T(8,128)(2,1)S(1)}, u32[]{:S(2)}, u32[]{:S(2)}) %collective-permute-start.12) | collective-permute-done | bytes 262176 | tf_op jit(solution)/shard_map/ppermute | solution.py:17
  143.1 3.6 %collective-permute-done.15 = bf16[6,1,128,128]{3,2,1,0:T(8,128)(2,1)S(1)} collective-permute-done((bf16[6,1,128,128]{3,2,1,0:T(8,128)(2,1)S(1)}, bf16[6,1,128,128]{3,2,1,0:T(8,128)(2,1)S(1)}, u32[]{:S(2)}, u32[]{:S(2)}) %collective-permute-start.15) | collective-permute-done | bytes 196640 | tf_op jit(solution)/shard_map/ppermute | solution.py:18
  146.7 2.1 %collective-permute-done.14 = bf16[6,1,128,128]{3,2,1,0:T(8,128)(2,1)S(1)} collective-permute-done((bf16[6,1,128,128]{3,2,1,0:T(8,128)(2,1)S(1)}, bf16[6,1,128,128]{3,2,1,0:T(8,128)(2,1)S(1)}, u32[]{:S(2)}, u32[]{:S(2)}) %collective-permute-start.14) | collective-permute-done | bytes 196640 | tf_op jit(solution)/shard_map/ppermute | solution.py:17
  150.7 3.7 %copy-done.2 = bf16[9,4,8,128,128]{4,3,2,1,0:T(8,128)(2,1)} copy-done((bf16[9,4,8,128,128]{4,3,2,1,0:T(8,128)(2,1)}, bf16[9,4,8,128,128]{4,3,2,1,0:T(8,128)(2,1)S(1)}, u32[]{:S(2)}) %copy-start.2) | copy-done | bytes 9437208
  154.3 8.4 %fusion.8 = f32[4,8,128,128]{3,2,1,0:T(8,128)} fusion(f32[4,8,128,128]{3,2,1,0:T(8,128)} %get-tuple-element.30, bf16[4,8,9,128,128]{4,3,2,1,0:T(8,128)(2,1)S(1)} %bitcast.178, bf16[9,4,8,128,128]{4,3,2,1,0:T(8,128)(2,1)} %copy-done.2), kind=kOutput, calls=%fused_computation.14 | convolution fusion | flops 1209008128 | bytes 23068672 | tf_op jit(solution)/shard_map/xyoij,oxyjm->xyim/dot_general | solution.py:47
  (79 shorter events, 40.5 us)
Async XLA Ops:
  0.0 10.9 %copy-start.1 = (bf16[4,8,128,128]{3,2,1,0:T(8,128)(2,1)S(1)}, bf16[4,8,128,128]{3,2,1,0:T(8,128)(2,1)}, u32[]{:S(2)}) copy-start(bf16[4,8,128,128]{3,2,1,0:T(8,128)(2,1)} %param.3) | copy-start | bytes 3145732
  1.2 12.0 %copy-start.3 = (s32[4,8,9]{2,1,0:T(8,128)S(1)}, s32[4,8,9]{2,1,0:T(8,128)}, u32[]{:S(2)}) copy-start(s32[4,8,9]{2,1,0:T(8,128)} %param.5) | copy-start | bytes 3460
  1.2 9.7 %collective-permute-start = (bf16[1,8,128,128]{3,2,1,0:T(8,128)(2,1)S(1)}, bf16[1,8,128,128]{3,2,1,0:T(8,128)(2,1)S(1)}, u32[]{:S(2)}, u32[]{:S(2)}) collective-permute-start(bf16[1,8,128,128]{3,2,1,0:T(8,128)(2,1)S(1)} %get-tuple-element.26), channel_id=1, source_target_pairs={{0,2},{2,4},{4,6},{6,8},{8,10},{10,12},{12,14},{14,16},{16,18},{18... | collective-permute-start | bytes 786440 | tf_op jit(solution)/shard_map/ppermute | solution.py:17
  1.7 9.3 %collective-permute-start.1 = (bf16[1,8,128,128]{3,2,1,0:T(8,128)(2,1)S(1)}, bf16[1,8,128,128]{3,2,1,0:T(8,128)(2,1)S(1)}, u32[]{:S(2)}, u32[]{:S(2)}) collective-permute-start(bf16[1,8,128,128]{3,2,1,0:T(8,128)(2,1)S(1)} %get-tuple-element.25), channel_id=1, source_target_pairs={{2,0},{4,2},{6,4},{8,6},{10,8},{12,10},{14,12},{16,14},{18,16},{20... | collective-permute-start | bytes 786440 | tf_op jit(solution)/shard_map/ppermute | solution.py:18
  11.1 23.6 %collective-permute-start.2 = (bf16[6,1,128,128]{3,2,1,0:T(8,128)(2,1)S(1)}, bf16[6,1,128,128]{3,2,1,0:T(8,128)(2,1)S(1)}, u32[]{:S(2)}, u32[]{:S(2)}) collective-permute-start(bf16[6,1,128,128]{3,2,1,0:T(8,128)(2,1)S(1)} %get-tuple-element.18), channel_id=1, source_target_pairs={{0,1},{1,0},{2,3},{3,2},{4,5},{5,4},{6,7},{7,6},{8,9},{9,8},{10,11... | collective-permute-start | bytes 589832 | tf_op jit(solution)/shard_map/ppermute | solution.py:17
  34.6 16.1 %copy-start = (bf16[4,8,9,128,128]{4,3,2,1,0:T(8,128)(2,1)}, bf16[4,8,9,128,128]{4,3,2,1,0:T(8,128)(2,1)S(1)}, u32[]{:S(2)}) copy-start(bf16[4,8,9,128,128]{4,3,2,1,0:T(8,128)(2,1)S(1)} %copy.47) | copy-start | bytes 28311556
  34.6 7.7 %collective-permute-start.3 = (bf16[6,1,128,128]{3,2,1,0:T(8,128)(2,1)S(1)}, bf16[6,1,128,128]{3,2,1,0:T(8,128)(2,1)S(1)}, u32[]{:S(2)}, u32[]{:S(2)}) collective-permute-start(bf16[6,1,128,128]{3,2,1,0:T(8,128)(2,1)S(1)} %get-tuple-element.17), channel_id=1, source_target_pairs={{1,0},{0,1},{3,2},{2,3},{5,4},{4,5},{7,6},{6,7},{9,8},{8,9},{11,10... | collective-permute-start | bytes 589832 | tf_op jit(solution)/shard_map/ppermute | solution.py:18
  58.4 8.7 %collective-permute-start.4 = (bf16[1,8,128,128]{3,2,1,0:T(8,128)(2,1)S(1)}, bf16[1,8,128,128]{3,2,1,0:T(8,128)(2,1)S(1)}, u32[]{:S(2)}, u32[]{:S(2)}) collective-permute-start(bf16[1,8,128,128]{3,2,1,0:T(8,128)(2,1)S(1)} %get-tuple-element.23), channel_id=1, source_target_pairs={{0,2},{2,4},{4,6},{6,8},{8,10},{10,12},{12,14},{14,16},{16,18},{18... | collective-permute-start | bytes 786440 | tf_op jit(solution)/shard_map/ppermute | solution.py:17
  58.6 8.5 %collective-permute-start.5 = (bf16[1,8,128,128]{3,2,1,0:T(8,128)(2,1)S(1)}, bf16[1,8,128,128]{3,2,1,0:T(8,128)(2,1)S(1)}, u32[]{:S(2)}, u32[]{:S(2)}) collective-permute-start(bf16[1,8,128,128]{3,2,1,0:T(8,128)(2,1)S(1)} %get-tuple-element.24), channel_id=1, source_target_pairs={{2,0},{4,2},{6,4},{8,6},{10,8},{12,10},{14,12},{16,14},{18,16},{20... | collective-permute-start | bytes 786440 | tf_op jit(solution)/shard_map/ppermute | solution.py:18
  67.1 7.8 %collective-permute-start.7 = (bf16[6,1,128,128]{3,2,1,0:T(8,128)(2,1)S(1)}, bf16[6,1,128,128]{3,2,1,0:T(8,128)(2,1)S(1)}, u32[]{:S(2)}, u32[]{:S(2)}) collective-permute-start(bf16[6,1,128,128]{3,2,1,0:T(8,128)(2,1)S(1)} %get-tuple-element.15), channel_id=1, source_target_pairs={{1,0},{0,1},{3,2},{2,3},{5,4},{4,5},{7,6},{6,7},{9,8},{8,9},{11,10... | collective-permute-start | bytes 589832 | tf_op jit(solution)/shard_map/ppermute | solution.py:18
  67.2 11.4 %collective-permute-start.6 = (bf16[6,1,128,128]{3,2,1,0:T(8,128)(2,1)S(1)}, bf16[6,1,128,128]{3,2,1,0:T(8,128)(2,1)S(1)}, u32[]{:S(2)}, u32[]{:S(2)}) collective-permute-start(bf16[6,1,128,128]{3,2,1,0:T(8,128)(2,1)S(1)} %get-tuple-element.16), channel_id=1, source_target_pairs={{0,1},{1,0},{2,3},{3,2},{4,5},{5,4},{6,7},{7,6},{8,9},{9,8},{10,11... | collective-permute-start | bytes 589832 | tf_op jit(solution)/shard_map/ppermute | solution.py:17
  78.5 10.1 %slice-start = ((s8[9437184]{0:T(1024)(128)(4,1)}), s8[4194304]{0:T(1024)(128)(4,1)S(1)}, s32[]{:S(2)}) async-start(s8[9437184]{0:T(1024)(128)(4,1)} %bitcast.177), calls=%async_computation | async-start | bytes 8388608
  80.2 8.5 %slice-start.1 = ((s8[9437184]{0:T(1024)(128)(4,1)}), s8[4194304]{0:T(1024)(128)(4,1)S(1)}, s32[]{:S(2)}) async-start(s8[9437184]{0:T(1024)(128)(4,1)} %bitcast.177), calls=%async_computation.1 | async-start | bytes 8388608
  84.4 4.2 %slice-start.2 = ((s8[9437184]{0:T(1024)(128)(4,1)}), s8[1048576]{0:T(1024)(128)(4,1)S(1)}, s32[]{:S(2)}) async-start(s8[9437184]{0:T(1024)(128)(4,1)} %bitcast.177), calls=%async_computation.2 | async-start | bytes 2097152
  96.5 8.5 %collective-permute-start.8 = (bf16[1,8,128,128]{3,2,1,0:T(8,128)(2,1)S(1)}, bf16[1,8,128,128]{3,2,1,0:T(8,128)(2,1)S(1)}, u32[]{:S(2)}, u32[]{:S(2)}) collective-permute-start(bf16[1,8,128,128]{3,2,1,0:T(8,128)(2,1)S(1)} %get-tuple-element.21), channel_id=1, source_target_pairs={{0,2},{2,4},{4,6},{6,8},{8,10},{10,12},{12,14},{14,16},{16,18},{18... | collective-permute-start | bytes 786440 | tf_op jit(solution)/shard_map/ppermute | solution.py:17
  96.6 8.5 %collective-permute-start.9 = (bf16[1,8,128,128]{3,2,1,0:T(8,128)(2,1)S(1)}, bf16[1,8,128,128]{3,2,1,0:T(8,128)(2,1)S(1)}, u32[]{:S(2)}, u32[]{:S(2)}) collective-permute-start(bf16[1,8,128,128]{3,2,1,0:T(8,128)(2,1)S(1)} %get-tuple-element.22), channel_id=1, source_target_pairs={{2,0},{4,2},{6,4},{8,6},{10,8},{12,10},{14,12},{16,14},{18,16},{20... | collective-permute-start | bytes 786440 | tf_op jit(solution)/shard_map/ppermute | solution.py:18
  105.1 7.7 %collective-permute-start.11 = (bf16[6,1,128,128]{3,2,1,0:T(8,128)(2,1)S(1)}, bf16[6,1,128,128]{3,2,1,0:T(8,128)(2,1)S(1)}, u32[]{:S(2)}, u32[]{:S(2)}) collective-permute-start(bf16[6,1,128,128]{3,2,1,0:T(8,128)(2,1)S(1)} %get-tuple-element.11), channel_id=1, source_target_pairs={{1,0},{0,1},{3,2},{2,3},{5,4},{4,5},{7,6},{6,7},{9,8},{8,9},{11,10... | collective-permute-start | bytes 589832 | tf_op jit(solution)/shard_map/ppermute | solution.py:18
  105.6 9.3 %collective-permute-start.10 = (bf16[6,1,128,128]{3,2,1,0:T(8,128)(2,1)S(1)}, bf16[6,1,128,128]{3,2,1,0:T(8,128)(2,1)S(1)}, u32[]{:S(2)}, u32[]{:S(2)}) collective-permute-start(bf16[6,1,128,128]{3,2,1,0:T(8,128)(2,1)S(1)} %get-tuple-element.12), channel_id=1, source_target_pairs={{0,1},{1,0},{2,3},{3,2},{4,5},{5,4},{6,7},{7,6},{8,9},{9,8},{10,11... | collective-permute-start | bytes 589832 | tf_op jit(solution)/shard_map/ppermute | solution.py:17
  132.4 8.5 %collective-permute-start.12 = (bf16[1,8,128,128]{3,2,1,0:T(8,128)(2,1)S(1)}, bf16[1,8,128,128]{3,2,1,0:T(8,128)(2,1)S(1)}, u32[]{:S(2)}, u32[]{:S(2)}) collective-permute-start(bf16[1,8,128,128]{3,2,1,0:T(8,128)(2,1)S(1)} %get-tuple-element.19), channel_id=1, source_target_pairs={{0,2},{2,4},{4,6},{6,8},{8,10},{10,12},{12,14},{14,16},{16,18},{18... | collective-permute-start | bytes 786440 | tf_op jit(solution)/shard_map/ppermute | solution.py:17
  132.4 8.5 %collective-permute-start.13 = (bf16[1,8,128,128]{3,2,1,0:T(8,128)(2,1)S(1)}, bf16[1,8,128,128]{3,2,1,0:T(8,128)(2,1)S(1)}, u32[]{:S(2)}, u32[]{:S(2)}) collective-permute-start(bf16[1,8,128,128]{3,2,1,0:T(8,128)(2,1)S(1)} %get-tuple-element.20), channel_id=1, source_target_pairs={{2,0},{4,2},{6,4},{8,6},{10,8},{12,10},{14,12},{16,14},{18,16},{20... | collective-permute-start | bytes 786440 | tf_op jit(solution)/shard_map/ppermute | solution.py:18
  141.0 5.7 %collective-permute-start.15 = (bf16[6,1,128,128]{3,2,1,0:T(8,128)(2,1)S(1)}, bf16[6,1,128,128]{3,2,1,0:T(8,128)(2,1)S(1)}, u32[]{:S(2)}, u32[]{:S(2)}) collective-permute-start(bf16[6,1,128,128]{3,2,1,0:T(8,128)(2,1)S(1)} %get-tuple-element.7), channel_id=1, source_target_pairs={{1,0},{0,1},{3,2},{2,3},{5,4},{4,5},{7,6},{6,7},{9,8},{8,9},{11,10... | collective-permute-start | bytes 589832 | tf_op jit(solution)/shard_map/ppermute | solution.py:18
  142.8 6.0 %collective-permute-start.14 = (bf16[6,1,128,128]{3,2,1,0:T(8,128)(2,1)S(1)}, bf16[6,1,128,128]{3,2,1,0:T(8,128)(2,1)S(1)}, u32[]{:S(2)}, u32[]{:S(2)}) collective-permute-start(bf16[6,1,128,128]{3,2,1,0:T(8,128)(2,1)S(1)} %get-tuple-element.8), channel_id=1, source_target_pairs={{0,1},{1,0},{2,3},{3,2},{4,5},{5,4},{6,7},{7,6},{8,9},{9,8},{10,11... | collective-permute-start | bytes 589832 | tf_op jit(solution)/shard_map/ppermute | solution.py:17
  150.7 3.7 %copy-start.2 = (bf16[9,4,8,128,128]{4,3,2,1,0:T(8,128)(2,1)}, bf16[9,4,8,128,128]{4,3,2,1,0:T(8,128)(2,1)S(1)}, u32[]{:S(2)}) copy-start(bf16[9,4,8,128,128]{4,3,2,1,0:T(8,128)(2,1)S(1)} %fusion.30) | copy-start | bytes 28311556
where the time goes:
time: 163 us
  matrix products  44.4 us (27%)
  waiting for transfers between devices  43.6 us (27%)
  local copies, waits for them, and re-layouts  30.3 us (19%)
  starting transfers between devices  27.5 us (17%)
  other arithmetic  16.7 us (10%)
    dot_general x4, matrix products, operate(): jnp.einsum('xyoij,oxyjm->xyim', ordered, stacked, preferred_element_type=...  31 us
    ppermute x8, waiting for transfers between devices, padded_2(): before = lax.ppermute(last, axis, up)  24.2 us
    ppermute x8, starting transfers between devices, padded_2(): after = lax.ppermute(first, axis, down)  20.7 us
    ppermute x8, waiting for transfers between devices, padded_2(): after = lax.ppermute(first, axis, down)  19.4 us
    unnamed x35, local copies, waits for them, and re-layouts  18.7 us
    unnamed x14, other arithmetic  13.7 us
    dot_general x1, matrix products, on_device(): jnp.einsum('xyko,xykij->xyoij', onehot, hamiltonian, preferred_element_ty...  13.4 us
    dot_general x1, local copies, waits for them, and re-layouts, on_device(): jnp.einsum('xyko,xykij->xyoij', onehot, hamiltonian, preferred_element_ty...  8.07 us
  transfers between devices with their start and end apart: 16, of which 11 were waited for; matrix products, arithmetic and copies ran while one was open for 15% of the time, Pallas kernels for 0%

commit v1 on v0

v1 whole, which is shorter than its diff:
```python
import functools

import jax
import jax.numpy as jnp
from jax import lax
from jax.experimental import pallas as pl
from jax.experimental.pallas import tpu as pltpu
from jax.sharding import PartitionSpec as P

STEPS = 4
NBR = 9
MESH = pl.DeviceIdType.MESH


def filter_kernel(nx, ny, nb_ref, v_hbm, h_hbm, out_hbm, vbuf, hbuf, ybuf, inv,
                  row_send, row_recv, col_send, col_recv, v_sem, h_sem, out_sem):
    rows, cols = v_hbm.shape[0], v_hbm.shape[1]
    gx, gy = lax.axis_index("gx"), lax.axis_index("gy")
    up = (lax.rem(gx + nx - 1, nx), gy)
    down = (lax.rem(gx + 1, nx), gy)
    left = (gx, lax.rem(gy + ny - 1, ny))
    right = (gx, lax.rem(gy + 1, ny))

    barrier = pltpu.get_barrier_semaphore()
    for neighbour in (up, down, left, right):
        pl.semaphore_signal(barrier, inc=1, device_id=neighbour, device_id_type=MESH)

    v_copy = pltpu.make_async_copy(v_hbm, vbuf.at[0, pl.ds(1, rows), pl.ds(1, cols)], v_sem)
    v_copy.start()
    h_copies = []
    for r in range(rows):
        h_copies.append(pltpu.make_async_copy(h_hbm.at[r], hbuf.at[r], h_sem.at[r]))
        h_copies[-1].start()

    def row_copy(slot, way, c, source=None):
        src_row, dst_row, device = ((1, rows + 1, up), (rows, 0, down))[way]
        src = vbuf.at[slot, src_row, c] if source is None else source
        return pltpu.make_async_remote_copy(
            src_ref=src, dst_ref=vbuf.at[slot, dst_row, c],
            send_sem=row_send.at[slot, way, c], recv_sem=row_recv.at[slot, way, c],
            device_id=device, device_id_type=MESH)

    def col_copy(slot, way, piece, source=None):
        src_col, dst_col, device = ((1, cols + 1, left), (cols, 0, right))[way]
        first, count = ((1, 1), (rows, 1), (2, rows - 2))[piece]
        src = vbuf.at[slot, pl.ds(first, count), src_col]
        if source is not None:
            src = source.at[pl.ds(first - 1, count), src_col - 1]
        return pltpu.make_async_remote_copy(
            src_ref=src, dst_ref=vbuf.at[slot, pl.ds(first, count), dst_col],
            send_sem=col_send.at[slot, way, piece], recv_sem=col_recv.at[slot, way, piece],
            device_id=device, device_id_type=MESH)

    order = []
    for j in range((cols + 1) // 2):
        order.append((j, cols - 1 - j) if j != cols - 1 - j else (j,))

    pl.semaphore_wait(barrier, 4)

    for piece in range(3):
        for way in range(2):
            col_copy(0, way, piece, v_hbm).start()
    for pair in order:
        for j in pair:
            row_copy(0, 0, j + 1, v_hbm.at[0, j]).start()
            row_copy(0, 1, j + 1, v_hbm.at[rows - 1, j]).start()

    def invert(cell, carry):
        r, c = cell // cols, cell % cols
        packed = jnp.int32(0)
        for k in range(NBR):
            code = nb_ref[r, c, k]
            packed = packed + jnp.where(code == NBR - 1, 0, jnp.int32(k) << ((code & 7) * 4))
        total = jnp.int32(0)
        for o in range(NBR - 1):
            entry = jnp.minimum(lax.shift_right_logical(packed, jnp.int32(4 * o)) & 15, NBR - 1)
            inv[cell * NBR + o] = entry
            total = total + entry
        inv[cell * NBR + NBR - 1] = jnp.clip(NBR * (NBR - 1) // 2 - total, 0, NBR - 1)
        return carry

    lax.fori_loop(0, rows * cols, invert, 0)

    v_copy.wait()

    def start_values(r, carry):
        for c in range(cols):
            ybuf[0, r, c] = vbuf[0, r + 1, c + 1].astype(jnp.float32)
            ybuf[1, r, c] = jnp.zeros(ybuf.shape[3:], jnp.float32)
        return carry

    lax.fori_loop(0, rows, start_values, 0)
    for copy in h_copies:
        copy.wait()

    def out_copy(r, c):
        return pltpu.make_async_copy(ybuf.at[0, r, c], out_hbm.at[r, c], out_sem.at[r, c])

    def step(k, last):
        factor = jnp.where(k == 0, 1.0, 2.0).astype(jnp.float32)
        kept = lax.rem(k + 1, 2)

        def cells(places):
            for r, c in places:
                base = (r * cols + c) * NBR
                lhs = jnp.concatenate([hbuf[r, c, inv[base + o]] for o in range(NBR)], axis=1)
                rhs = jnp.concatenate(
                    [vbuf[k, r + o // 3, c + o % 3] for o in range(NBR)], axis=0)
                acc = jnp.dot(lhs, rhs, preferred_element_type=jnp.float32)
                new = factor * acc - ybuf[kept, r, c]
                ybuf[kept, r, c] = new
                if not last:
                    vbuf[k + 1, r + 1, c + 1] = new.astype(jnp.bfloat16)
            if last:
                for r, c in places:
                    out_copy(r, c).start()

        for piece in range(2):
            for way in range(2):
                col_copy(k, way, piece).wait_recv()
        for way in range(2):
            row_copy(k, way, 0).start()
            row_copy(k, way, cols + 1).start()
        for c in range(1, cols - 1):
            cells([(r, c) for r in range(1, rows - 1)])
        for way in range(2):
            col_copy(k, way, 2).wait_recv()
        cells([(r, j) for j in order[0] for r in range(1, rows - 1)])
        if not last:
            for way in range(2):
                col_copy(k + 1, way, 2).start()
        waited = set()
        for number, pair in enumerate(order):
            for j in pair:
                for c in (j, j + 1, j + 2):
                    if c not in waited:
                        waited.add(c)
                        for way in range(2):
                            row_copy(k, way, c).wait_recv()
            cells([(r, j) for j in pair for r in (0, rows - 1)])
            if not last:
                if number == 0:
                    for piece in range(2):
                        for way in range(2):
                            col_copy(k + 1, way, piece).start()
                for j in pair:
                    for way in range(2):
                        row_copy(k + 1, way, j + 1).start()

    def looped(k, carry):
        step(k, False)
        return carry

    lax.fori_loop(0, STEPS - 1, looped, 0)
    step(STEPS - 1, True)

    def drain(k, carry):
        for way in range(2):
            for c in range(cols + 2):
                row_copy(k, way, c).wait_send()
            for piece in range(3):
                col_copy(k, way, piece).wait_send()
        return carry

    lax.fori_loop(0, STEPS, drain, 0)
    for r in range(rows):
        for c in range(cols):
            out_copy(r, c).wait()


def on_device(nx, ny, vectors, hamiltonian, neighbours):
    rows, cols, height, width = vectors.shape
    return pl.pallas_call(
        functools.partial(filter_kernel, nx, ny),
        out_shape=jax.ShapeDtypeStruct(vectors.shape, jnp.float32),
        in_specs=[
            pl.BlockSpec(memory_space=pltpu.SMEM),
            pl.BlockSpec(memory_space=pl.ANY),
            pl.BlockSpec(memory_space=pl.ANY),
        ],
        out_specs=pl.BlockSpec(memory_space=pl.ANY),
        scratch_shapes=[
            pltpu.VMEM((STEPS, rows + 2, cols + 2, height, width), jnp.bfloat16),
            pltpu.VMEM(hamiltonian.shape, jnp.bfloat16),
            pltpu.VMEM((2,) + vectors.shape, jnp.float32),
            pltpu.SMEM((rows * cols * NBR,), jnp.int32),
            pltpu.SemaphoreType.DMA((STEPS, 2, cols + 2)),
            pltpu.SemaphoreType.DMA((STEPS, 2, cols + 2)),
            pltpu.SemaphoreType.DMA((STEPS, 2, 3)),
            pltpu.SemaphoreType.DMA((STEPS, 2, 3)),
            pltpu.SemaphoreType.DMA,
            pltpu.SemaphoreType.DMA((rows,)),
            pltpu.SemaphoreType.DMA((rows, cols)),
        ],
        compiler_params=pltpu.CompilerParams(
            collective_id=0, has_side_effects=True, vmem_limit_bytes=60 * 1024 * 1024),
    )(neighbours, vectors, hamiltonian)


def solution(mesh):
    placed = (P("gx", "gy", None, None), P("gx", "gy", None, None, None), P("gx", "gy", None))
    return jax.shard_map(
        functools.partial(on_device, mesh.shape["gx"], mesh.shape["gy"]),
        mesh=mesh, in_specs=placed, out_specs=P("gx", "gy", None, None), check_vma=False
    )
```

time: 163 us -> 49.2 us (0.30)
  Pallas kernels: 0 us -> 45.8 us
  matrix products: 44.4 us -> 0 us
  waiting for transfers between devices: 43.6 us -> 0 us
  starting transfers between devices: 27.5 us -> 0 us
  local copies, waits for them, and re-layouts: 30.3 us -> 3.14 us
  other arithmetic: 16.7 us -> 0 us
    pallas_call x0 -> x1, Pallas kernels: none -> 45.8 us  [on_device(): pl.pallas_call(functools.partial(filter_kernel, nx, ny), out_shape=jax.Sh...]
    dot_general x5 -> x0, matrix products: 44.4 us -> none  [the longest x4 31 us: operate(): jnp.einsum('xyoij,oxyjm->xyim', ordered, stacked, preferred_element_type=...]
    ppermute x16 -> x0, waiting for transfers between devices: 43.6 us -> none  [the longest x8 24.2 us: padded_2(): before = lax.ppermute(last, axis, up)]
    ppermute x16 -> x0, starting transfers between devices: 27.5 us -> none  [the longest x8 20.7 us: padded_2(): after = lax.ppermute(first, axis, down)]
    unnamed x35 -> x1, local copies, waits for them, and re-layouts: 18.7 us -> 3.14 us
    unnamed x14 -> x0, other arithmetic: 13.7 us -> none
    dot_general x1 -> x0, local copies, waits for them, and re-layouts: 8.07 us -> none  [on_device(): jnp.einsum('xyko,xykij->xyoij', onehot, hamiltonian, preferred_element_ty...]
    another operation x3 -> x0, local copies, waits for them, and re-layouts: 2.24 us -> none  [neighbour_stack(): return jnp.stack(views, axis=0)]
  transfers between devices with their start and end apart: 16 -> 0, of which waited for: 11 -> 0; matrix products, arithmetic and copies ran while one was open for 15% -> 0% of each run, Pallas kernels for 0% -> 0%
where the time goes in v1:
time: 49.2 us; the launch traced here: 48.9 us
  Pallas kernels  45.8 us (93%)
  local copies, waits for them, and re-layouts  3.14 us (6%)
    pallas_call x1, Pallas kernels, on_device(): pl.pallas_call(functools.partial(filter_kernel, nx, ny), out_shape=jax.Sh...  45.8 us
    unnamed x1, local copies, waits for them, and re-layouts  3.14 us

profile of v1, /device:TPU:0, one launch (start us, length us, event | category | flops | bytes accessed | tf_op | source)
XLA Modules:
  0.0 48.9 jit_solution(8962037658887060226)
XLA Ops:
  0.0 45.8 %shard_map.37 = f32[4,8,128,128]{3,2,1,0:T(8,128)} custom-call(s32[4,8,9]{2,1,0:T(8,128)} %nb_ref.1, bf16[4,8,128,128]{3,2,1,0:T(8,128)(2,1)} %v_hbm.1, bf16[4,8,9,128,128]{4,3,2,1,0:T(8,128)(2,1)} %h_hbm.1), custom_call_target="tpu_custom_call" | custom-call | tf_op jit(solution)/shard_map/pallas_call | solution.py:173
  45.8 3.1 %copy.5 = f32[4,8,128,128]{3,2,1,0:T(8,128)} copy(f32[4,8,128,128]{3,2,1,0:T(8,128)} %shard_map.37) | data formatting | bytes 4194304

commit v2 on v1

--- a/solution.py
+++ b/solution.py
@@ -21,8 +21,18 @@
     left = (gx, lax.rem(gy + ny - 1, ny))
     right = (gx, lax.rem(gy + 1, ny))
 
+    parity = lax.rem(gx, 2)
+    across = jnp.where(parity == 0, up[0], down[0])
+    diagonals = ((across, left[1]), (across, right[1]))
+
+    mirrored = lax.rem(gy, 2) == 1
+
+    def at(p, length):
+        return jnp.where(mirrored, length - 1 - p, p)
+
+    near_send = jnp.where(mirrored, 1, 0)
     barrier = pltpu.get_barrier_semaphore()
-    for neighbour in (up, down, left, right):
+    for neighbour in (up, down, left, right) + diagonals:
         pl.semaphore_signal(barrier, inc=1, device_id=neighbour, device_id_type=MESH)
 
     v_copy = pltpu.make_async_copy(v_hbm, vbuf.at[0, pl.ds(1, rows), pl.ds(1, cols)], v_sem)
@@ -40,8 +50,32 @@
             send_sem=row_send.at[slot, way, c], recv_sem=row_recv.at[slot, way, c],
             device_id=device, device_id_type=MESH)
 
+    def ends(way):
+        return (jnp.where(way == 0, 1, cols), jnp.where(way == 0, cols + 1, 0),
+                jnp.where(way == 0, left[1], right[1]))
+
+    def diagonal_copy(slot, way, side_way, source=None):
+        src_row, dst_row = ((1, rows + 1), (rows, 0))[way]
+        src_col, dst_col, place = ends(side_way)
+        src = vbuf.at[slot, src_row, src_col]
+        if source is not None:
+            src = source.at[src_row - 1, src_col - 1]
+        return pltpu.make_async_remote_copy(
+            src_ref=src, dst_ref=vbuf.at[slot, dst_row, dst_col],
+            send_sem=row_send.at[slot, way, dst_col], recv_sem=row_recv.at[slot, way, dst_col],
+            device_id=(across, place), device_id_type=MESH)
+
+    def send_corner(slot, side, source=None):
+        for way in range(2):
+            @pl.when(parity == way)
+            def _():
+                diagonal_copy(slot, way, send_way(side), source).start()
+
+    def send_way(side):
+        return near_send if side == 0 else 1 - near_send
+
     def col_copy(slot, way, piece, source=None):
-        src_col, dst_col, device = ((1, cols + 1, left), (cols, 0, right))[way]
+        src_col, dst_col, place = ends(way)
         first, count = ((1, 1), (rows, 1), (2, rows - 2))[piece]
         src = vbuf.at[slot, pl.ds(first, count), src_col]
         if source is not None:
@@ -49,21 +83,29 @@
         return pltpu.make_async_remote_copy(
             src_ref=src, dst_ref=vbuf.at[slot, pl.ds(first, count), dst_col],
             send_sem=col_send.at[slot, way, piece], recv_sem=col_recv.at[slot, way, piece],
-            device_id=device, device_id_type=MESH)
-
-    order = []
-    for j in range((cols + 1) // 2):
-        order.append((j, cols - 1 - j) if j != cols - 1 - j else (j,))
-
-    pl.semaphore_wait(barrier, 4)
-
-    for piece in range(3):
+            device_id=(gx, place), device_id_type=MESH)
+
+    half = (cols + 1) // 2
+    halves = (tuple(range(half)), tuple(range(cols - 1, half - 1, -1)))
+
+    pl.semaphore_wait(barrier, 6)
+
+    def pass_corner(slot, side):
+        place = at(0 if side == 0 else cols + 1, cols + 2)
         for way in range(2):
-            col_copy(0, way, piece, v_hbm).start()
-    for pair in order:
-        for j in pair:
+            @pl.when(parity != way)
+            def _():
+                row_copy(slot, way, place).start()
+
+    for side in range(2):
+        send_corner(0, side, v_hbm)
+        for number, p in enumerate(halves[side]):
+            j = at(p, cols)
             row_copy(0, 0, j + 1, v_hbm.at[0, j]).start()
             row_copy(0, 1, j + 1, v_hbm.at[rows - 1, j]).start()
+            if number == 0:
+                for piece in range(3):
+                    col_copy(0, send_way(side), piece, v_hbm).start()
 
     def invert(cell, carry):
         r, c = cell // cols, cell % cols
@@ -115,37 +157,40 @@
                 for r, c in places:
                     out_copy(r, c).start()
 
-        for piece in range(2):
-            for way in range(2):
-                col_copy(k, way, piece).wait_recv()
-        for way in range(2):
-            row_copy(k, way, 0).start()
-            row_copy(k, way, cols + 1).start()
-        for c in range(1, cols - 1):
-            cells([(r, c) for r in range(1, rows - 1)])
-        for way in range(2):
-            col_copy(k, way, 2).wait_recv()
-        cells([(r, j) for j in order[0] for r in range(1, rows - 1)])
-        if not last:
-            for way in range(2):
-                col_copy(k + 1, way, 2).start()
         waited = set()
-        for number, pair in enumerate(order):
-            for j in pair:
-                for c in (j, j + 1, j + 2):
-                    if c not in waited:
-                        waited.add(c)
-                        for way in range(2):
-                            row_copy(k, way, c).wait_recv()
-            cells([(r, j) for j in pair for r in (0, rows - 1)])
+
+        def rim(p, side=None):
+            j = at(p, cols)
+            for q in (p, p + 1, p + 2):
+                if q not in waited:
+                    waited.add(q)
+                    for way in range(2):
+                        row_copy(k, way, at(q, cols + 2)).wait_recv()
+            cells([(0, j), (rows - 1, j)])
             if not last:
-                if number == 0:
+                if side is not None:
+                    send_corner(k + 1, side)
                     for piece in range(2):
-                        for way in range(2):
-                            col_copy(k + 1, way, piece).start()
-                for j in pair:
-                    for way in range(2):
-                        row_copy(k + 1, way, j + 1).start()
+                        col_copy(k + 1, send_way(side), piece).start()
+                for way in range(2):
+                    row_copy(k + 1, way, j + 1).start()
+
+        for side in range(2):
+            edge = halves[side][0]
+            for piece in range(2):
+                col_copy(k, 1 - send_way(side), piece).wait_recv()
+            pass_corner(k, side)
+            col_copy(k, 1 - send_way(side), 2).wait_recv()
+            cells([(r, at(edge, cols)) for r in range(1, rows - 1)])
+            if not last:
+                col_copy(k + 1, send_way(side), 2).start()
+            rim(edge, side)
+            for p in halves[side][1:]:
+                rim(p)
+
+        for side in range(2):
+            for p in halves[side][1:]:
+                cells([(r, at(p, cols)) for r in range(1, rows - 1)])
 
     def looped(k, carry):
         step(k, False)

time: 49.2 us -> 47.1 us (0.957)
  Pallas kernels: 45.8 us -> 43.3 us
    pallas_call x1, Pallas kernels: 45.8 us -> 43.3 us  [on_device(): pl.pallas_call(functools.partial(filter_kernel, nx, ny), out_shape=jax.Sh...]
where the time goes in v2:
time: 47.1 us; the launch traced here: 46.5 us
  Pallas kernels  43.3 us (92%)
  local copies, waits for them, and re-layouts  3.14 us (7%)
    pallas_call x1, Pallas kernels, on_device(): pl.pallas_call(functools.partial(filter_kernel, nx, ny), out_shape=jax.Sh...  43.3 us
    unnamed x1, local copies, waits for them, and re-layouts  3.14 us

profile of v2, /device:TPU:0, one launch (start us, length us, event | category | flops | bytes accessed | tf_op | source)
XLA Modules:
  0.0 46.5 jit_solution(11064399157486768195)
XLA Ops:
  0.0 43.3 %shard_map.37 = f32[4,8,128,128]{3,2,1,0:T(8,128)} custom-call(s32[4,8,9]{2,1,0:T(8,128)} %nb_ref.1, bf16[4,8,128,128]{3,2,1,0:T(8,128)(2,1)} %v_hbm.1, bf16[4,8,9,128,128]{4,3,2,1,0:T(8,128)(2,1)} %h_hbm.1), custom_call_target="tpu_custom_call" | custom-call | tf_op jit(solution)/shard_map/pallas_call | solution.py:218
  43.4 3.1 %copy.5 = f32[4,8,128,128]{3,2,1,0:T(8,128)} copy(f32[4,8,128,128]{3,2,1,0:T(8,128)} %shard_map.37) | data formatting | bytes 4194304
